TPU v7x, 256 devices: a whole 4x4x8 slice. The times are simulated.
256 devices in a mesh: dp: 8 (over y, core), seq: 32 (over z, x).
Axes of the slice: x: 4, y: 4, z: 8, core: 2. Of those that a mesh axis runs over, the one named last changes fastest.
Arguments:
- queries: bfloat16 [8, 16384, 1024], P('dp', 'seq'), may hold values from -6 to 6
- keys: bfloat16 [8, 16384, 1024], P('dp', 'seq'), may hold values from -6 to 6
- values: bfloat16 [8, 16384, 1024], P('dp', 'seq'), may hold values from -6 to 6
- out_grad: bfloat16 [8, 16384, 2048], P('dp', 'seq'), may hold values from -6 to 6
- out_weight: bfloat16 [1024, 2048], P(('dp', 'seq')), may hold values from -0.125 to 0.125
- gain: float32 [1024], replicated, may hold values from 0.1 to 1.9
Outputs:
- query_grad: bfloat16 [8, 16384, 1024], P('dp', 'seq')
- key_grad: bfloat16 [8, 16384, 1024], P('dp', 'seq')
- value_grad: bfloat16 [8, 16384, 1024], P('dp', 'seq')
- weight_grad: float32 [1024, 2048], P(('dp', 'seq'))
- gain_grad: float32 [1024], replicated
All inputs are finite; a program needn't handle non-finite values.
Results may differ from a plain program's by a relative error of at most 0.015.
Values may be sent and summed in bfloat16 or wider, within the bound.
A program may use at most 128 MiB of HBM per device.

v0:
```python
import jax
import jax.numpy as jnp
from jax import lax
from jax.sharding import PartitionSpec as P

HEADS = 8
HEAD_DIM = 128
BLOCK = 512
HD = 1024
norm_eps = 1e-06


def prefix(x, axis, combine, identity, reverse):
    peers, here = (lax.axis_size(axis), lax.axis_index(axis))
    everything = lax.all_gather(x, axis)
    start = jnp.broadcast_to(jnp.asarray(identity, x.dtype), x.shape)

    def hop(k, before):
        at = peers - 1 - k if reverse else k
        reached = at > here if reverse else at < here
        new = combine(before, everything[at])
        return jnp.where(reached, new, before)

    return lax.fori_loop(0, peers, hop, start)


def causal_mask():
    places = jnp.arange(BLOCK, dtype=jnp.int32)
    return (places[None, :] <= places[:, None]).astype(jnp.float32)


def add_states(earlier, later):
    return earlier + later


def before_each(block_terms):
    running = jnp.cumsum(block_terms, axis=0)
    return jnp.concatenate([jnp.zeros_like(block_terms), running[:-1]], axis=0)


def after_each(block_terms):
    running = jnp.cumsum(block_terms[::-1], axis=0)[::-1]
    return jnp.concatenate([running[1:], jnp.zeros_like(block_terms)], axis=0)


def shards(queries, keys, values, out_grad, out_weight, gain):
    tok_count = queries.shape[1]
    blocks = tok_count // BLOCK
    block_shape = (blocks, BLOCK, HEADS, HEAD_DIM)
    query_blk = queries.reshape(block_shape)
    key_blk = keys.reshape(block_shape)
    value_blk = values.reshape(block_shape)
    grad_rows = out_grad[0]
    gain_heads = gain.reshape(HEADS, HEAD_DIM)
    causal = causal_mask()
    state_zero = jnp.zeros((HEADS, HEAD_DIM, HEAD_DIM), jnp.float32)
    block_kv = jnp.einsum("nshd,nshe->nhde", key_blk, value_blk, preferred_element_type=jnp.float32)
    within = before_each(block_kv)
    local_total = jnp.sum(block_kv, axis=0)
    before = prefix(local_total, "seq", add_states, state_zero, False)
    state_bf = (before[None] + within).astype(jnp.bfloat16)
    scores = jnp.einsum("nthd,nshd->nhts", query_blk, key_blk, preferred_element_type=jnp.float32)
    attn_bf = (scores * causal[None, None]).astype(jnp.bfloat16)
    outputs = jnp.einsum("nhts,nshd->nthd", attn_bf, value_blk, preferred_element_type=jnp.float32)
    outputs = outputs + jnp.einsum(
        "nthd,nhde->nthe", query_blk, state_bf, preferred_element_type=jnp.float32
    )
    rms = jnp.sqrt(jnp.mean(outputs * outputs, axis=-1, keepdims=True) + norm_eps)
    normed = outputs / rms
    unit_bf = (normed * gain_heads[None, None]).astype(jnp.bfloat16)
    unit_grad = lax.dot_general(
        grad_rows,
        lax.all_gather(out_weight, ("dp", "seq"), axis=0, tiled=True),
        (((1,), (1,)), ((), ())),
        preferred_element_type=jnp.float32,
    ).reshape(block_shape)
    gain_part = jnp.sum(unit_grad * normed, axis=(0, 1)).reshape(-1)
    scaled = unit_grad * gain_heads[None, None]
    middle = jnp.mean(scaled * normed, axis=-1, keepdims=True)
    attn_grad = ((scaled - normed * middle) / rms).astype(jnp.bfloat16)
    block_qg = jnp.einsum(
        "nthd,nthe->nhde", query_blk, attn_grad, preferred_element_type=jnp.float32
    )
    later_inside = after_each(block_qg)
    local_qg = jnp.sum(block_qg, axis=0)
    after = prefix(local_qg, "seq", add_states, state_zero, True)
    rev_bf = (after[None] + later_inside).astype(jnp.bfloat16)
    score_grad = (
        jnp.einsum("nthe,nshe->nhts", attn_grad, value_blk, preferred_element_type=jnp.float32)
        * causal[None, None]
    ).astype(jnp.bfloat16)
    query_g = jnp.einsum("nhts,nshd->nthd", score_grad, key_blk, preferred_element_type=jnp.float32)
    query_g = query_g + jnp.einsum(
        "nthe,nhde->nthd", attn_grad, state_bf, preferred_element_type=jnp.float32
    )
    key_g = jnp.einsum("nhts,nthd->nshd", score_grad, query_blk, preferred_element_type=jnp.float32)
    key_g = key_g + jnp.einsum(
        "nshe,nhde->nshd", value_blk, rev_bf, preferred_element_type=jnp.float32
    )
    value_g = jnp.einsum("nhts,nthe->nshe", attn_bf, attn_grad, preferred_element_type=jnp.float32)
    value_g = value_g + jnp.einsum(
        "nshd,nhde->nshe", key_blk, rev_bf, preferred_element_type=jnp.float32
    )
    unit_flat = unit_bf.reshape(tok_count, HD)
    data_count = lax.axis_size("dp")
    seq_count = lax.axis_size("seq")
    weight_sum = lax.psum_scatter(
        lax.dot_general(
            unit_flat, grad_rows, (((0,), (0,)), ((), ())), preferred_element_type=jnp.float32
        ),
        ("dp", "seq"),
        scatter_dimension=0,
        tiled=True,
    )
    gain_total = lax.psum(gain_part, ("dp", "seq"))
    factor = 1.0 / jnp.sqrt(jnp.float32(tok_count * data_count * seq_count))
    out_shape = (1, tok_count, HD)
    return (
        query_g.astype(jnp.bfloat16).reshape(out_shape),
        key_g.astype(jnp.bfloat16).reshape(out_shape),
        value_g.astype(jnp.bfloat16).reshape(out_shape),
        weight_sum * factor,
        gain_total * factor,
    )


def solution(mesh):
    placed = (
        P("dp", "seq", None),
        P("dp", "seq", None),
        P("dp", "seq", None),
        P("dp", "seq", None),
        P(("dp", "seq"), None),
        P(),
    )
    return jax.shard_map(
        shards,
        mesh=mesh,
        in_specs=placed,
        out_specs=(
            P("dp", "seq", None),
            P("dp", "seq", None),
            P("dp", "seq", None),
            P(("dp", "seq"), None),
            P(),
        ),
        check_vma=False,
    )
```

profile of v0, /device:TPU:1, one launch (start us, length us, event | category | flops | bytes accessed | tf_op | source)
XLA Modules:
  0.0 829.1 jit_solution(12613035057772357722)
XLA Ops:
  8.0 1.5 copy.61
  9.5 1.5 copy.37
  10.9 1.6 copy.62
  12.5 1.2 fusion.20
  13.9 1.6 copy.60
  16.8 3.3 multiply_convert_fusion.1
  20.1 111.6 %all-gather.11.cloned.1.call-done = bf16[256,4,2048]{2,1,0:T(4,128)(2,1)} async-done(((bf16[1,4,2048]{2,1,0:T(4,128)(2,1)}), bf16[256,4,2048]{2,1,0:T(4,128)(2,1)}) %all-gather.11.cloned.1.call-update) | async-done | bytes 4194320 | tf_op jit(solution)/shard_map/all_gather | solution.py:73
  131.7 6.9 reshape.183
  138.6 5.9 fusion.5
  144.5 126.3 %all-gather.7.cloned.1.call-done = f32[256,128,128]{2,1,0:T(8,128)} async-done(((f32[8,128,128]{2,1,0:T(8,128)}), f32[256,128,128]{2,1,0:T(8,128)}) %all-gather.7.cloned.1.call-update) | async-done | bytes 16777232 | tf_op jit(solution)/shard_map/all_gather | solution.py:15
  270.8 65.3 %while.30 = (s32[]{:T(128)}, f32[8,128,128]{2,1,0:T(8,128)}, s32[]{:T(128)}, f32[32,8,128,128]{3,2,1,0:T(8,128)}, s32[]{:T(128)}, /*index=5*/s32[]{:T(128)}) while((s32[]{:T(128)}, f32[8,128,128]{2,1,0:T(8,128)}, s32[]{:T(128)}, f32[32,8,128,128]{3,2,1,0:T(8,128)}, s32[]{:T(128)}, /*index=5*/s32[]{:T(128)}) %tuple.92), condition=%wide.region_1.2_spmd.clone, body=%wide.region_0.0_spmd.clone.sunk | while | flops 393220 | bytes 1572957 | solution.py:24
  270.8 1.9 add_select_fusion.4
  272.7 2.0 add_select_fusion.4
  274.7 2.0 add_select_fusion.4
  276.8 2.0 add_select_fusion.4
  278.8 2.0 add_select_fusion.4
  280.9 2.0 add_select_fusion.4
  282.9 2.0 add_select_fusion.4
  285.0 2.0 add_select_fusion.4
  287.0 2.0 add_select_fusion.4
  289.0 2.0 add_select_fusion.4
  291.1 2.0 add_select_fusion.4
  293.1 2.0 add_select_fusion.4
  295.2 2.0 add_select_fusion.4
  297.2 2.0 add_select_fusion.4
  299.3 2.0 add_select_fusion.4
  301.3 2.0 add_select_fusion.4
  303.4 2.0 add_select_fusion.4
  305.4 2.0 add_select_fusion.4
  307.5 2.0 add_select_fusion.4
  309.5 2.0 add_select_fusion.4
  311.5 2.0 add_select_fusion.4
  313.6 2.0 add_select_fusion.4
  315.6 2.0 add_select_fusion.4
  317.7 2.0 add_select_fusion.4
  319.7 2.0 add_select_fusion.4
  321.8 2.0 add_select_fusion.4
  323.8 2.0 add_select_fusion.4
  325.9 2.0 add_select_fusion.4
  327.9 2.0 add_select_fusion.4
  329.9 2.0 add_select_fusion.4
  332.0 2.0 add_select_fusion.4
  334.0 2.0 add_select_fusion.4
  336.1 1.9 fusion.25
  338.0 3.8 fusion.2
  342.7 1.6 multiply_convert_fusion.2
  344.3 5.6 fusion.3
  351.5 1.2 convolution_bitcast_fusion
  352.7 2.1 copy.47
  354.8 1.5 fusion.10
  356.4 1.4 multiply_convert_fusion
  357.8 2.5 fusion.1
  360.2 2.3 copy.52
  362.5 76.0 %psum.7 = f32[1024]{0:T(1024)S(1)} all-reduce(f32[1024]{0:T(1024)S(1)} %bitcast.111), channel_id=1, replica_groups=mesh['dp'=8,'seq'=32] {'dp','seq'}, use_global_device_ids=true, to_apply=%region_8.9 | all-reduce | flops 1024 | bytes 8192 | tf_op jit(solution)/shard_map/psum | solution.py:115
  439.1 4.3 fusion.7
  443.4 183.4 %all-reduce.3.cloned.1.call-done = f32[1024,2048]{1,0:T(8,128)} async-done(((f32[1024,2048]{1,0:T(8,128)}), f32[1024,2048]{1,0:T(8,128)}) %all-reduce.3.cloned.1.call-update) | async-done | bytes 8388624
  626.7 1.5 dynamic-slice_multiply_fusion
  628.2 140.6 %all-gather.9.cloned.1.call-done = f32[256,128,128]{2,1,0:T(8,128)} async-done(((f32[8,128,128]{2,1,0:T(8,128)}), f32[256,128,128]{2,1,0:T(8,128)}) %all-gather.9.cloned.1.call-update) | async-done | bytes 16777232 | tf_op jit(solution)/shard_map/all_gather | solution.py:15
  768.8 40.2 %while.31 = (s32[]{:T(128)}, f32[8,128,128]{2,1,0:T(8,128)S(1)}, s32[]{:T(128)}, f32[32,8,128,128]{3,2,1,0:T(8,128)}, s32[]{:T(128)}, /*index=5*/s32[]{:T(128)}, s32[]{:T(128)}, s32[]{:T(128)}) while((s32[]{:T(128)}, f32[8,128,128]{2,1,0:T(8,128)S(1)}, s32[]{:T(128)}, f32[32,8,128,128]{3,2,1,0:T(8,128)}, s32[]{:T(128)}, ...), condition=%wide.region_5.6_spmd.clone, body=%wide.region_4.5_spmd.clone.sunk | while | flops 393224 | bytes 1573019 | solution.py:24
  809.0 1.8 fusion.17
  811.7 1.5 add_convert_fusion
  813.2 2.4 copy.54
  815.5 4.8 fusion
  820.3 2.3 copy.53
  (81 shorter events, 45.3 us)
Async XLA Ops:
  7.2 131.5 %copy-start = (bf16[1,512,2048]{2,1,0:T(8,128)(2,1)S(1)}, bf16[1,512,2048]{2,1,0:T(8,128)(2,1)}, u32[]{:S(2)}) copy-start(bf16[1,512,2048]{2,1,0:T(8,128)(2,1)} %param.13) | copy-start | bytes 6291460
  7.2 124.5 %all-gather.11.cloned.1.call-start = ((), (), s32[]{:S(2)}) async-start(), calls=%async_computation.2 | async-start | bytes 4210688 | tf_op jit(solution)/shard_map/all_gather | solution.py:73
  7.9 262.9 %all-gather.7.cloned.1.call-start = ((), (), s32[]{:S(2)}) async-start(), calls=%async_computation | async-start | bytes 17301504 | tf_op jit(solution)/shard_map/all_gather | solution.py:15
  9.5 1.5 copy-start.7
  10.9 1.6 copy-start.12
  13.8 612.9 %all-reduce.3.cloned.1.call-start = ((), (), s32[]{:S(2)}) async-start(), calls=%async_computation.3 | async-start | bytes 16777216
  13.9 2.9 copy-start.8
  15.5 1.0 copy-start.4
  15.6 1.2 copy-start.10
  338.0 3.9 copy-start.15
  338.0 3.9 copy-start.16
  349.9 1.2 copy-start.3
  349.9 1.5 copy-start.5
  349.9 418.8 %all-gather.9.cloned.1.call-start = ((), (), s32[]{:S(2)}) async-start(), calls=%async_computation.1 | async-start | bytes 17301504 | tf_op jit(solution)/shard_map/all_gather | solution.py:15
  354.8 1.6 copy-start.11
  356.4 1.4 copy-start.13
  357.8 2.5 copy-start.2
  809.0 1.8 copy-start.9
  809.0 2.7 copy-start.14
  813.2 2.4 copy-start.6
  815.5 7.0 copy-start.1
Sparse Core Ops, SparseCore 0:
  11.7 119.9 all-gather.10
  134.9 135.9 all-gather.6
  350.1 276.6 all-reduce.2
  629.2 139.5 all-gather.8
where the time goes:
time: 832 us; the launch traced here: 829 us
  waiting for transfers between devices  562 us (68%)
  other arithmetic  109 us (13%)
  blocking collectives  76 us (9%)
  matrix products  40.8 us (5%)
  local copies, waits for them, and re-layouts  25.4 us (3%)
  between operations  14 us (2%)
    all_gather x2, waiting for transfers between devices, prefix(): everything = lax.all_gather(x, axis)  267 us
    unnamed x5, waiting for transfers between devices  184 us
    all_gather x1, waiting for transfers between devices, shards(): lax.all_gather(out_weight, ('dp', 'seq'), axis=0, tiled=True)  112 us
    select_n x64, other arithmetic, hop(): return jnp.where(reached, new, before)  105 us
    psum x1, blocking collectives, shards(): gain_total = lax.psum(gain_part, ('dp', 'seq'))  76 us
    unnamed x41, local copies, waits for them, and re-layouts  21.9 us
  transfers between devices with their start and end apart: 4, of which 4 were waited for; matrix products, arithmetic and copies ran while one was open for 5% of the time, Pallas kernels for 0%

commit v1 on v0

--- a/solution.py
+++ b/solution.py
@@ -112,7 +112,9 @@
         scatter_dimension=0,
         tiled=True,
     )
-    gain_total = lax.psum(gain_part, ("dp", "seq"))
+    gain_total = gain_part
+    for over in ("dp", "seq"):
+        gain_total = lax.psum(gain_total, over)
     factor = 1.0 / jnp.sqrt(jnp.float32(tok_count * data_count * seq_count))
     out_shape = (1, tok_count, HD)
     return (

time: 832 us -> 832 us (level)
    psum x1 -> x2, blocking collectives: 76 us -> 71 us  [shards(): gain_total = lax.psum(gain_total, over)]
where the time goes in v1:
time: 832 us; the launch traced here: 829 us
  waiting for transfers between devices  567 us (68%)
  other arithmetic  110 us (13%)
  blocking collectives  71 us (9%)
  matrix products  40.8 us (5%)
  local copies, waits for them, and re-layouts  25.4 us (3%)
  between operations  14 us (2%)
    all_gather x2, waiting for transfers between devices, prefix(): everything = lax.all_gather(x, axis)  267 us
    unnamed x5, waiting for transfers between devices  189 us
    all_gather x1, waiting for transfers between devices, shards(): lax.all_gather(out_weight, ('dp', 'seq'), axis=0, tiled=True)  112 us
    select_n x64, other arithmetic, hop(): return jnp.where(reached, new, before)  105 us
    psum x2, blocking collectives, shards(): gain_total = lax.psum(gain_total, over)  71 us
    unnamed x41, local copies, waits for them, and re-layouts  21.9 us
  transfers between devices with their start and end apart: 4, of which 4 were waited for; matrix products, arithmetic and copies ran while one was open for 5% of the time, Pallas kernels for 0%

profile of v1, /device:TPU:1, one launch (start us, length us, event | category | flops | bytes accessed | tf_op | source)
XLA Modules:
  0.0 829.2 jit_solution(17557568287463174366)
XLA Ops:
  8.0 1.5 copy.61
  9.5 1.5 copy.37
  10.9 1.6 copy.62
  13.9 1.6 copy.60
  16.8 3.3 multiply_convert_fusion.1
  20.1 111.6 %all-gather.11.cloned.1.call-done = bf16[256,4,2048]{2,1,0:T(4,128)(2,1)} async-done(((bf16[1,4,2048]{2,1,0:T(4,128)(2,1)}), bf16[256,4,2048]{2,1,0:T(4,128)(2,1)}) %all-gather.11.cloned.1.call-update) | async-done | bytes 4194320 | tf_op jit(solution)/shard_map/all_gather | solution.py:73
  131.7 7.0 reshape.183
  138.7 5.9 fusion.5
  144.5 126.3 %all-gather.7.cloned.1.call-done = f32[256,128,128]{2,1,0:T(8,128)} async-done(((f32[8,128,128]{2,1,0:T(8,128)}), f32[256,128,128]{2,1,0:T(8,128)}) %all-gather.7.cloned.1.call-update) | async-done | bytes 16777232 | tf_op jit(solution)/shard_map/all_gather | solution.py:15
  270.8 65.7 %while.30 = (s32[]{:T(128)}, f32[8,128,128]{2,1,0:T(8,128)}, s32[]{:T(128)}, f32[32,8,128,128]{3,2,1,0:T(8,128)}, s32[]{:T(128)}, /*index=5*/s32[]{:T(128)}) while((s32[]{:T(128)}, f32[8,128,128]{2,1,0:T(8,128)}, s32[]{:T(128)}, f32[32,8,128,128]{3,2,1,0:T(8,128)}, s32[]{:T(128)}, /*index=5*/s32[]{:T(128)}) %tuple.92), condition=%wide.region_1.2_spmd.clone, body=%wide.region_0.0_spmd.clone.sunk | while | flops 393220 | bytes 1572957 | solution.py:24
  270.8 1.9 add_select_fusion.4
  272.7 2.1 add_select_fusion.4
  274.8 2.1 add_select_fusion.4
  276.8 2.1 add_select_fusion.4
  278.9 2.1 add_select_fusion.4
  280.9 2.1 add_select_fusion.4
  283.0 2.1 add_select_fusion.4
  285.1 2.1 add_select_fusion.4
  287.1 2.1 add_select_fusion.4
  289.2 2.1 add_select_fusion.4
  291.2 2.1 add_select_fusion.4
  293.3 2.1 add_select_fusion.4
  295.3 2.1 add_select_fusion.4
  297.4 2.1 add_select_fusion.4
  299.5 2.1 add_select_fusion.4
  301.5 2.1 add_select_fusion.4
  303.6 2.1 add_select_fusion.4
  305.6 2.1 add_select_fusion.4
  307.7 2.1 add_select_fusion.4
  309.7 2.1 add_select_fusion.4
  311.8 2.1 add_select_fusion.4
  313.9 2.1 add_select_fusion.4
  315.9 2.1 add_select_fusion.4
  318.0 2.1 add_select_fusion.4
  320.0 2.1 add_select_fusion.4
  322.1 2.1 add_select_fusion.4
  324.2 2.1 add_select_fusion.4
  326.2 2.1 add_select_fusion.4
  328.3 2.1 add_select_fusion.4
  330.3 2.1 add_select_fusion.4
  332.4 2.1 add_select_fusion.4
  334.4 2.1 add_select_fusion.4
  336.5 1.9 fusion.25
  338.4 3.8 fusion.2
  343.2 1.6 multiply_convert_fusion.2
  344.8 5.6 fusion.3
  351.9 1.3 convolution_bitcast_fusion
  353.1 2.1 copy.47
  355.2 1.5 fusion.10
  356.8 1.4 multiply_convert_fusion
  358.2 2.5 fusion.1
  360.7 2.3 copy.52
  362.9 13.2 %psum.14 = f32[1024]{0:T(1024)S(1)} all-reduce(f32[1024]{0:T(1024)S(1)} %bitcast.111), channel_id=1, replica_groups=mesh['dp'=8,'seq'=32] {'dp'}, use_global_device_ids=true, to_apply=%region_8.9 | all-reduce | flops 1024 | bytes 8192 | tf_op jit(solution)/shard_map/psum | solution.py:117
  376.1 57.8 %psum.15 = f32[1024]{0:T(1024)S(1)} all-reduce(f32[1024]{0:T(1024)S(1)} %psum.14), channel_id=1, replica_groups=mesh['dp'=8,'seq'=32] {'seq'}, use_global_device_ids=true, to_apply=%region_9.10 | all-reduce | flops 1024 | bytes 8192 | tf_op jit(solution)/shard_map/psum | solution.py:117
  434.5 4.3 fusion.7
  438.8 188.0 %all-reduce.3.cloned.1.call-done = f32[1024,2048]{1,0:T(8,128)} async-done(((f32[1024,2048]{1,0:T(8,128)}), f32[1024,2048]{1,0:T(8,128)}) %all-reduce.3.cloned.1.call-update) | async-done | bytes 8388624
  626.8 1.5 dynamic-slice_multiply_fusion
  628.3 140.6 %all-gather.9.cloned.1.call-done = f32[256,128,128]{2,1,0:T(8,128)} async-done(((f32[8,128,128]{2,1,0:T(8,128)}), f32[256,128,128]{2,1,0:T(8,128)}) %all-gather.9.cloned.1.call-update) | async-done | bytes 16777232 | tf_op jit(solution)/shard_map/all_gather | solution.py:15
  768.8 40.2 %while.31 = (s32[]{:T(128)}, f32[8,128,128]{2,1,0:T(8,128)S(1)}, s32[]{:T(128)}, f32[32,8,128,128]{3,2,1,0:T(8,128)}, s32[]{:T(128)}, /*index=5*/s32[]{:T(128)}, s32[]{:T(128)}, s32[]{:T(128)}) while((s32[]{:T(128)}, f32[8,128,128]{2,1,0:T(8,128)S(1)}, s32[]{:T(128)}, f32[32,8,128,128]{3,2,1,0:T(8,128)}, s32[]{:T(128)}, ...), condition=%wide.region_5.6_spmd.clone, body=%wide.region_4.5_spmd.clone.sunk | while | flops 393224 | bytes 1573019 | solution.py:24
  809.1 1.8 fusion.17
  811.8 1.5 add_convert_fusion
  813.3 2.4 copy.54
  815.6 4.8 fusion
  820.4 2.3 copy.53
  (82 shorter events, 46.5 us)
Async XLA Ops:
  7.2 131.5 %copy-start = (bf16[1,512,2048]{2,1,0:T(8,128)(2,1)S(1)}, bf16[1,512,2048]{2,1,0:T(8,128)(2,1)}, u32[]{:S(2)}) copy-start(bf16[1,512,2048]{2,1,0:T(8,128)(2,1)} %param.13) | copy-start | bytes 6291460
  7.2 124.5 %all-gather.11.cloned.1.call-start = ((), (), s32[]{:S(2)}) async-start(), calls=%async_computation.2 | async-start | bytes 4210688 | tf_op jit(solution)/shard_map/all_gather | solution.py:73
  7.9 262.9 %all-gather.7.cloned.1.call-start = ((), (), s32[]{:S(2)}) async-start(), calls=%async_computation | async-start | bytes 17301504 | tf_op jit(solution)/shard_map/all_gather | solution.py:15
  9.5 1.5 copy-start.7
  10.9 1.6 copy-start.12
  13.8 613.0 %all-reduce.3.cloned.1.call-start = ((), (), s32[]{:S(2)}) async-start(), calls=%async_computation.3 | async-start | bytes 16777216
  13.9 2.9 copy-start.8
  15.5 1.0 copy-start.4
  15.6 1.2 copy-start.10
  338.4 3.9 copy-start.15
  338.4 3.9 copy-start.16
  350.3 1.2 copy-start.3
  350.3 1.5 copy-start.5
  350.4 418.5 %all-gather.9.cloned.1.call-start = ((), (), s32[]{:S(2)}) async-start(), calls=%async_computation.1 | async-start | bytes 17301504 | tf_op jit(solution)/shard_map/all_gather | solution.py:15
  355.2 1.6 copy-start.11
  356.8 1.4 copy-start.13
  358.2 2.5 copy-start.2
  809.1 1.8 copy-start.9
  809.1 2.7 copy-start.14
  813.3 2.4 copy-start.6
  815.6 7.0 copy-start.1
Sparse Core Ops, SparseCore 0:
  11.7 119.9 all-gather.10
  134.9 135.9 all-gather.6
  350.5 276.2 all-reduce.2
  629.3 139.5 all-gather.8
